TPU v7x, 32 devices: a whole 2x2x4 slice. The times are simulated.
32 devices in a mesh: dp: 8 (over z, x), head: 4 (over y, core).
Axes of the slice: x: 2, y: 2, z: 4, core: 2. Of those that a mesh axis runs over, the one named last changes fastest.
Arguments:
- layer_input: bfloat16 [64, 197, 768], P(('dp', 'head')), may hold values from -6 to 6
- prompts: bfloat16 [100, 768], replicated, may hold values from -6 to 6
- lengths: int32 [64], P('dp'), may hold values from 1 to 100, as said below
- key_mask: int32 [64, 297], P('dp'), may hold values 0 or 1
- ln1_gain: float32 [768], replicated, may hold values from 0.1 to 1.9
- ln1_shift: float32 [768], replicated, may hold values from -1.5 to 1.5
- w_qkv: bfloat16 [3, 768, 768], P(None, 'dp', 'head'), may hold values from -0.3125 to 0.3125
- w_out: bfloat16 [768, 768], P('head', 'dp'), may hold values from -0.875 to 0.875
- b_out: float32 [768], replicated, may hold values from -1.5 to 1.5
- ln2_gain: float32 [768], replicated, may hold values from 0.1 to 1.9
- ln2_shift: float32 [768], replicated, may hold values from -1.5 to 1.5
- w_fc1: bfloat16 [768, 3072], P('dp', 'head'), may hold values from -0.21875 to 0.21875
- b_fc1: float32 [3072], P('head'), may hold values from -2.5 to 2.5
- w_fc2: bfloat16 [3072, 768], P('head', 'dp'), may hold values from -0.15625 to 0.15625
- b_fc2: float32 [768], replicated, may hold values from -1.5 to 1.5
- grad_output: bfloat16 [64, 297, 768], P(('dp', 'head')), may hold values from -6 to 6
Outputs:
- layer_output: bfloat16 [64, 297, 768], P(('dp', 'head'))
- grad_input: bfloat16 [64, 197, 768], P(('dp', 'head'))
- grad_prompts: float32 [100, 768], replicated
Inputs may be any that keep to these rules, and one draw needn't show every extreme that they name: `lengths`: each length is one of 1, 10, 50 and 100; both 1 and 100 occur.
All inputs are finite; a program needn't handle non-finite values. No bound on the sum of `key_mask` on one device may be relied on, other than what follows from the above.
Results may differ from a plain program's by a relative error of at most 0.019.
Values may be sent and summed in bfloat16 or wider, within the bound.
No kernel may reach another device: no remote copies, remote signals or barrier semaphores. Data moves between devices by JAX's collectives and lax.ppermute only.
A program may use at most 128 MiB of HBM per device.

v0:
```python
import jax
import jax.numpy as jnp
from jax import lax
from jax.sharding import PartitionSpec as P

HEAD_DIM = 64
IMG_TOK = 197
PROMPTS = 100
EPSILON = 1e-06


def layer_norm(rows, gain, shift):
    center = rows - jnp.mean(rows, axis=-1, keepdims=True)
    return (
        center * lax.rsqrt(jnp.mean(center * center, axis=-1, keepdims=True) + EPSILON) * gain
        + shift
    )


def token_masks(lengths, key_mask):
    position = lax.broadcasted_iota(jnp.int32, key_mask.shape, 1)
    used = (position < IMG_TOK) | (position - IMG_TOK < lengths[:, None])
    seen = (key_mask == 1) | (position == 0)
    return (used, used & seen)


def project(rows_b, weight):
    return jnp.einsum("isd,dc->isc", rows_b, weight, preferred_element_type=jnp.float32)


def attend(rows_b, full_qkv, visible):
    img_count, seq_len = (rows_b.shape[0], rows_b.shape[1])
    head_count = full_qkv.shape[2] // HEAD_DIM
    projected = jnp.einsum(
        "isd,tdc->tisc", rows_b, full_qkv, preferred_element_type=jnp.float32
    ).astype(jnp.bfloat16)
    projected = projected.reshape(3, img_count, seq_len, head_count, HEAD_DIM)
    query_rows, key_rows, value_rows = (projected[0], projected[1], projected[2])
    scores = jnp.einsum(
        "ishc,ithc->ihst", query_rows, key_rows, preferred_element_type=jnp.float32
    ) * HEAD_DIM ** (-0.5)
    scores = jnp.where(visible[:, None, None, :], scores, -1000000000.0)
    attn_probs = jax.nn.softmax(scores, axis=-1)
    return (query_rows, key_rows, value_rows, attn_probs)


def mix_values(probs_b, value_rows):
    img_count, seq_len = (value_rows.shape[0], value_rows.shape[1])
    context = jnp.einsum("ihst,ithc->ishc", probs_b, value_rows, preferred_element_type=jnp.float32)
    return context.astype(jnp.bfloat16).reshape(img_count, seq_len, value_rows.shape[2] * HEAD_DIM)


def mlp_back(grad_all, pre_act, fc1_rows, fc2_rows):
    grad_active_b = jnp.einsum(
        "isd,fd->isf", grad_all, fc2_rows, preferred_element_type=jnp.float32
    ).astype(jnp.bfloat16)
    _, gelu_back = jax.vjp(lambda values_in: jax.nn.gelu(values_in, approximate=False), pre_act)
    grad_pre_b = gelu_back(grad_active_b.astype(jnp.float32))[0].astype(jnp.bfloat16)
    return jnp.einsum("isf,df->isd", grad_pre_b, fc1_rows, preferred_element_type=jnp.float32)


def attn_back(grad_all, out_rows, qkv_rows, query_rows, key_rows, value_rows, attn_probs, probs_b):
    img_count, seq_len, head_count = (value_rows.shape[0], value_rows.shape[1], value_rows.shape[2])
    local_width = head_count * HEAD_DIM
    grad_context = jnp.einsum(
        "isd,cd->isc", grad_all, out_rows, preferred_element_type=jnp.float32
    ).astype(jnp.bfloat16)
    grad_context = grad_context.reshape(img_count, seq_len, head_count, HEAD_DIM)
    grad_value = jnp.einsum(
        "ihst,ishc->ithc", probs_b, grad_context, preferred_element_type=jnp.float32
    ).astype(jnp.bfloat16)
    grad_probs = jnp.einsum(
        "ishc,ithc->ihst", grad_context, value_rows, preferred_element_type=jnp.float32
    )
    grad_scores = (
        attn_probs * (grad_probs - jnp.sum(attn_probs * grad_probs, axis=-1, keepdims=True))
    ).astype(jnp.bfloat16)
    grad_query = (
        jnp.einsum("ihst,ithc->ishc", grad_scores, key_rows, preferred_element_type=jnp.float32)
        * HEAD_DIM ** (-0.5)
    ).astype(jnp.bfloat16)
    grad_key = (
        jnp.einsum("ihst,ishc->ithc", grad_scores, query_rows, preferred_element_type=jnp.float32)
        * HEAD_DIM ** (-0.5)
    ).astype(jnp.bfloat16)
    stacked = jnp.stack([grad_query, grad_key, grad_value]).reshape(
        3, img_count, seq_len, local_width
    )
    return jnp.einsum("tisc,tdc->isd", stacked, qkv_rows, preferred_element_type=jnp.float32)


def per_device(
    layer_input,
    prompts,
    lengths,
    key_mask,
    ln1_gain,
    ln1_shift,
    w_qkv,
    w_out,
    b_out,
    ln2_gain,
    ln2_shift,
    w_fc1,
    b_fc1,
    w_fc2,
    b_fc2,
    grad_output,
):
    own_count = layer_input.shape[0]
    model_width = layer_input.shape[2]
    offset = lax.axis_index("head") * own_count
    used_all, visible = token_masks(lengths, key_mask)
    used_own = lax.dynamic_slice_in_dim(used_all, offset, own_count, 0).astype(jnp.float32)[
        ..., None
    ]
    gain_one, shift_one = (ln1_gain, ln1_shift)
    gain_two, shift_two = (ln2_gain, ln2_shift)
    full_qkv, full_out, full_fc1, full_fc2 = (
        lax.all_gather(w_qkv, "dp", axis=1, tiled=True),
        lax.all_gather(w_out, "dp", axis=1, tiled=True),
        lax.all_gather(w_fc1, "dp", axis=0, tiled=True),
        lax.all_gather(w_fc2, "dp", axis=1, tiled=True),
    )
    prompt_rows = jnp.broadcast_to(
        prompts.astype(jnp.float32)[None], (own_count, PROMPTS, model_width)
    )
    stream = jnp.concatenate([layer_input.astype(jnp.float32), prompt_rows], axis=1)
    normed_attn, back_attn_norm = jax.vjp(
        lambda rows: layer_norm(rows, gain_one, shift_one), stream
    )
    normed_attn_b = normed_attn.astype(jnp.bfloat16)
    grad_rows = grad_output.astype(jnp.float32) * used_own
    gathered_attn = lax.all_gather(normed_attn_b, "head", axis=0, tiled=True)
    query_rows, key_rows, value_rows, attn_probs = attend(gathered_attn, full_qkv, visible)
    probs_b = attn_probs.astype(jnp.bfloat16)
    context = mix_values(probs_b, value_rows)
    attn_sum = lax.psum_scatter(
        project(context, full_out).astype(jnp.bfloat16), "head", scatter_dimension=0, tiled=True
    ).astype(jnp.float32)
    hidden_mid = stream + attn_sum + b_out
    normed_mlp, back_mlp_norm = jax.vjp(
        lambda rows: layer_norm(rows, gain_two, shift_two), hidden_mid
    )
    normed_mlp_b = normed_mlp.astype(jnp.bfloat16)
    gathered_mlp = lax.all_gather(normed_mlp_b, "head", axis=0, tiled=True)
    pre_act = project(gathered_mlp, full_fc1) + b_fc1
    active_b = jax.nn.gelu(pre_act, approximate=False).astype(jnp.bfloat16)
    mlp_sum = lax.psum_scatter(
        project(active_b, full_fc2).astype(jnp.bfloat16), "head", scatter_dimension=0, tiled=True
    ).astype(jnp.float32)
    result = ((hidden_mid + mlp_sum + b_fc2) * used_own).astype(jnp.bfloat16)
    held_inputs = lax.optimization_barrier((w_qkv, w_out, w_fc1, w_fc2, grad_rows))
    grad_rows = held_inputs[4]
    back_qkv, back_out, back_fc1, back_fc2 = (
        lax.all_gather(held_inputs[0], "dp", axis=1, tiled=True),
        lax.all_gather(held_inputs[1], "dp", axis=1, tiled=True),
        lax.all_gather(held_inputs[2], "dp", axis=0, tiled=True),
        lax.all_gather(held_inputs[3], "dp", axis=1, tiled=True),
    )
    grad_mlp_b = grad_rows.astype(jnp.bfloat16)
    grad_mlp_all, gathered_again = (
        lax.all_gather(grad_mlp_b, "head", axis=0, tiled=True),
        lax.all_gather(normed_mlp_b, "head", axis=0, tiled=True),
    )
    pre_act = project(gathered_again, back_fc1) + b_fc1
    grad_normed_mlp = lax.psum_scatter(
        mlp_back(grad_mlp_all, pre_act, back_fc1, back_fc2).astype(jnp.bfloat16),
        "head",
        scatter_dimension=0,
        tiled=True,
    ).astype(jnp.float32)
    grad_mid = grad_rows + back_mlp_norm(grad_normed_mlp)[0]
    grad_attn_b = grad_mid.astype(jnp.bfloat16)
    grad_attn_all, gathered_again = (
        lax.all_gather(grad_attn_b, "head", axis=0, tiled=True),
        lax.all_gather(normed_attn_b, "head", axis=0, tiled=True),
    )
    query_rows, key_rows, value_rows, attn_probs = attend(gathered_again, back_qkv, visible)
    probs_b = attn_probs.astype(jnp.bfloat16)
    grad_partial = attn_back(
        grad_attn_all, back_out, back_qkv, query_rows, key_rows, value_rows, attn_probs, probs_b
    )
    grad_normed_attn = lax.psum_scatter(
        grad_partial.astype(jnp.bfloat16), "head", scatter_dimension=0, tiled=True
    ).astype(jnp.float32)
    grad_stream = grad_mid + back_attn_norm(grad_normed_attn)[0]
    grad_input = grad_stream[:, :IMG_TOK].astype(jnp.bfloat16)
    grad_prompts = lax.psum(jnp.sum(grad_stream[:, IMG_TOK:], axis=0), ("dp", "head"))
    return (result, grad_input, grad_prompts)


def solution(mesh):
    placed = (
        P(("dp", "head"), None, None),
        P(),
        P("dp"),
        P("dp", None),
        P(),
        P(),
        P(None, "dp", "head"),
        P("head", "dp"),
        P(),
        P(),
        P(),
        P("dp", "head"),
        P("head"),
        P("head", "dp"),
        P(),
        P(("dp", "head"), None, None),
    )
    return jax.shard_map(
        per_device,
        mesh=mesh,
        in_specs=placed,
        out_specs=(P(("dp", "head"), None, None), P(("dp", "head"), None, None), P()),
        check_vma=False,
    )
```

profile of v0, /device:TPU:8, one launch (start us, length us, event | category | flops | bytes accessed | tf_op | source)
XLA Modules:
  0.0 717.3 jit_solution(3644398181313778874)
XLA Ops:
  8.1 1.2 copy_convert_fusion
  9.2 1.0 broadcast_in_dim.26
  10.2 0.2 fusion.72
  10.4 0.4 multiply_reduce_fusion.4
  10.9 1.3 add_convert_fusion.1
  12.4 0.1 copy.34
  12.6 36.7 %all_gather.39 = bf16[3,768,192]{2,0,1:T(4,128)(2,1)} all-gather(bf16[3,96,192]{2,0,1:T(4,128)(2,1)S(1)} %copy.34), channel_id=1, replica_groups=mesh['dp'=8,'head'=4] {'dp'}, dimensions={1}, use_global_device_ids=true | all-gather | bytes 995328 | tf_op jit(solution)/shard_map/all_gather | solution.py:120
  49.3 3.4 copy.35
  52.7 30.5 %all_gather.40 = bf16[192,768]{0,1:T(8,128)(2,1)S(1)} all-gather(bf16[192,96]{0,1:T(8,128)(2,1)S(1)} %copy.37), channel_id=1, replica_groups=mesh['dp'=8,'head'=4] {'dp'}, dimensions={1}, use_global_device_ids=true | all-gather | bytes 331776 | tf_op jit(solution)/shard_map/all_gather | solution.py:121
  83.3 5.2 convert_bitcast_fusion.1
  88.6 1.9 fusion.167
  90.5 8.2 %fusion.168 = (f32[8,3,297]{2,1,0:T(4,128)S(1)}, f32[8,3,297,297]{2,3,1,0:T(8,128)}) fusion(pred[8,297]{1,0:T(8,128)(4,1)S(1)} %get-tuple-element.30, bf16[8,297,3,64]{1,3,2,0:T(8,128)(2,1)} %bitcast.105, bf16[8,297,3,64]{1,3,2,0:T(8,128)(2,1)} %bitcast.104), kind=kOutput, calls=%fused_computation.222 | convolution fusion | flops 279446432 | bytes 10323720 | tf_op jit(solution)/shard_map/sub | solution.py:43
  98.7 5.8 fusion.73
  104.4 3.2 convolution_convert_fusion
  107.8 1.1 copy-done.9
  108.8 1.5 convert_multiply_fusion.4
  110.4 41.4 %reduce-scatter.5.cloned.1.call-done = bf16[2,297,768]{2,1,0:T(8,128)(2,1)} async-done(((bf16[8,297,768]{2,1,0:T(8,128)(2,1)}), bf16[2,297,768]{2,1,0:T(8,128)(2,1)}) %reduce-scatter.5.cloned.1.call-update) | async-done | bytes 912400 | tf_op jit(solution)/shard_map/reduce_scatter | solution.py:138
  151.8 1.6 fusion.165
  153.4 1.7 multiply_reduce_fusion.3
  155.1 1.5 add_convert_fusion
  156.7 0.5 all-gather.21.cloned.1.call-update
  157.3 2.6 convert_element_type.129
  159.9 0.7 all-gather.13.cloned.1.call-update
  160.7 0.7 all-gather.15.cloned.1.call-update
  161.4 0.3 reduce-scatter.9.cloned.1.call-start
  161.7 26.8 %all-gather.11.cloned.1.call-done = bf16[8,297,768]{2,1,0:T(8,128)(2,1)} async-done(((bf16[2,297,768]{2,1,0:T(8,128)(2,1)}), bf16[8,297,768]{2,1,0:T(8,128)(2,1)}) %all-gather.11.cloned.1.call-update) | async-done | bytes 3649552 | tf_op jit(solution)/shard_map/all_gather | solution.py:146
  188.5 8.4 %fusion.82 = f32[8,297,768]{2,1,0:T(8,128)} fusion(bf16[8,297,768]{2,1,0:T(8,128)(2,1)} %all-gather.11.cloned.1.call-done, bf16[768,768]{1,0:T(8,128)(2,1)} %all-gather.17.cloned.1.call-done), kind=kOutput, calls=%fused_computation.120 | convolution fusion | flops 2802843648 | bytes 12128256 | tf_op jit(solution)/shard_map/isd,dc->isc/dot_general | solution.py:28
  196.9 34.4 %all-gather.21.cloned.1.call-done = bf16[768,768]{0,1:T(8,128)(2,1)} async-done(((bf16[768,96]{0,1:T(8,128)(2,1)}), bf16[768,768]{0,1:T(8,128)(2,1)}) %all-gather.21.cloned.1.call-update) | async-done | bytes 1179664 | tf_op jit(solution)/shard_map/all_gather | solution.py:159
  231.3 32.9 %all-gather.19.cloned.1.call-done = bf16[8,297,768]{2,1,0:T(8,128)(2,1)} async-done(((bf16[2,297,768]{2,1,0:T(8,128)(2,1)}), bf16[8,297,768]{2,1,0:T(8,128)(2,1)}) %all-gather.19.cloned.1.call-update) | async-done | bytes 3649552 | tf_op jit(solution)/shard_map/all_gather | solution.py:163
  264.2 27.0 %fusion.57 = bf16[8,297,768]{2,1,0:T(8,128)(2,1)} fusion(f32[8,297,768]{2,1,0:T(8,128)} %fusion.82, f32[768]{0:T(1024)S(1)} %copy-done.35, bf16[8,297,768]{2,1,0:T(8,128)(2,1)} %all-gather.19.cloned.1.call-done, bf16[768,768]{0,1:T(8,128)(2,1)} %all-gather.21.cloned.1.call-done, bf16[768,768]{1,0:T(8,128)(2,1)} %all-gather.17.cloned.1.call-done), kind=kOutput, calls=%fused_computation.89 | convolution fusion | flops 5744369664 | bytes 16960512 | tf_op jit(solution)/shard_map/isf,df->isd/dot_general | solution.py:59
  291.2 9.2 %reduce-scatter.7.cloned.1.call-start = ((), (), s32[]{:S(2)}) async-start(), calls=%async_computation.9 | async-start | bytes 4669440 | tf_op jit(solution)/shard_map/reduce_scatter | solution.py:149
  300.4 6.6 all-gather.13.cloned.1.call-done
  307.0 10.3 %fusion.70 = (u8[297,768]{1,0:T(8,128)(4,1)S(1)}, u8[297,768]{1,0:T(8,128)(4,1)S(1)}, f32[8,297,768]{2,1,0:T(8,128)}) fusion(f32[768]{0:T(1024)S(1)} %copy-done.35, bf16[8,297,768]{2,1,0:T(8,128)(2,1)} %all-gather.11.cloned.1.call-done, bf16[768,768]{1,0:T(8,128)(2,1)} %all-gather.13.cloned.1.call-done), kind=kOutput, calls=%fused_computation.109 | convolution fusion | flops 2827934208 | bytes 12587520 | tf_op jit(solution)/shard_map/isd,dc->isc/dot_general | solution.py:28
  317.2 32.0 %all-gather.15.cloned.1.call-done = bf16[768,768]{0,1:T(8,128)(2,1)} async-done(((bf16[768,96]{0,1:T(8,128)(2,1)}), bf16[768,768]{0,1:T(8,128)(2,1)}) %all-gather.15.cloned.1.call-update) | async-done | bytes 1179664 | tf_op jit(solution)/shard_map/all_gather | solution.py:123
  349.3 23.0 %fusion.60 = bf16[8,297,768]{2,1,0:T(8,128)(2,1)} fusion(f32[8,297,768]{2,1,0:T(8,128)} %get-tuple-element.33, f32[768]{0:T(1024)S(1)} %copy-done.35, bf16[768,768]{0,1:T(8,128)(2,1)} %all-gather.15.cloned.1.call-done, u8[297,768]{1,0:T(8,128)(4,1)S(1)} %get-tuple-element.20, u8[297,768]{1,0:T(8,128)(4,1)S(1)} %get-tuple-element.19), kind=kOutput, calls=%fused_computation.90 | convolution fusion | flops 2934226944 | bytes 12587520 | tf_op jit(solution)/shard_map/isd,dc->isc/dot_general | solution.py:28
  372.4 1.9 multiply_reduce_fusion.2
  374.4 1.0 fusion.91
  375.4 38.2 %reduce-scatter.7.cloned.1.call-done = bf16[2,297,768]{2,1,0:T(8,128)(2,1)} async-done(((bf16[8,297,768]{2,1,0:T(8,128)(2,1)}), bf16[2,297,768]{2,1,0:T(8,128)(2,1)}) %reduce-scatter.7.cloned.1.call-update) | async-done | bytes 912400 | tf_op jit(solution)/shard_map/reduce_scatter | solution.py:149
  413.6 3.6 fusion.164
  417.5 28.5 %all_gather.49 = bf16[192,768]{0,1:T(8,128)(2,1)S(1)} all-gather(bf16[192,96]{0,1:T(8,128)(2,1)S(1)} %copy.42), channel_id=1, replica_groups=mesh['dp'=8,'head'=4] {'dp'}, dimensions={1}, use_global_device_ids=true | all-gather | bytes 331776 | tf_op jit(solution)/shard_map/all_gather | solution.py:157
  446.1 39.4 %all_gather.47 = bf16[3,768,192]{2,0,1:T(4,128)(2,1)S(1)} all-gather(bf16[3,96,192]{2,0,1:T(4,128)(2,1)S(1)} %copy.40), channel_id=1, replica_groups=mesh['dp'=8,'head'=4] {'dp'}, dimensions={1}, use_global_device_ids=true | all-gather | bytes 995328 | tf_op jit(solution)/shard_map/all_gather | solution.py:156
  485.5 7.7 %convert_bitcast_fusion = bf16[3,8,297,192]{2,3,1,0:T(8,128)(2,1)S(1)} fusion(bf16[8,297,768]{2,1,0:T(8,128)(2,1)} %all-gather.9.cloned.1.call-done, bf16[3,768,192,1]{2,0,1,3:T(4,128)(2,1)S(1)} %bitcast.101), kind=kOutput, calls=%fused_computation.84 | convolution fusion | flops 2103501312 | bytes 7271424 | tf_op jit(solution)/shard_map/isd,tdc->tisc/dot_general | solution.py:34
  493.2 2.0 fusion.166
  495.2 8.2 %fusion.169 = (f32[8,3,297]{2,1,0:T(4,128)S(1)}, f32[8,3,297,297]{2,3,1,0:T(8,128)}) fusion(pred[8,297]{1,0:T(8,128)(4,1)S(1)} %copy-done.33, bf16[8,297,3,64]{1,3,2,0:T(8,128)(2,1)} %bitcast.98, bf16[8,297,3,64]{1,3,2,0:T(8,128)(2,1)} %bitcast.96), kind=kOutput, calls=%fused_computation.223 | convolution fusion | flops 279446432 | bytes 10323720 | tf_op jit(solution)/shard_map/sub | solution.py:43
  503.5 3.6 convolution_convert_fusion.1
  507.1 7.6 %fusion.74 = bf16[8,3,64,297]{3,2,1,0:T(8,128)(2,1)} fusion(bf16[8,297,3,64]{1,3,2,0:T(8,128)(2,1)S(1)} %bitcast.109, f32[8,3,297,297]{2,3,1,0:T(8,128)} %get-tuple-element.35, f32[8,3,297]{2,1,0:T(4,128)S(1)} %get-tuple-element.34), kind=kOutput, calls=%fused_computation.113 | convolution fusion | flops 275668288 | bytes 10321344 | tf_op jit(solution)/shard_map/ihst,ishc->ithc/dot_general | solution.py:69
  514.8 3.4 multiply_reduce_fusion
  518.2 1.7 multiply_convert_fusion
  519.9 3.3 multiply_convert_fusion.1
  523.2 1.2 multiply_convert_fusion.2
  524.4 0.2 copy-done.8
  524.6 0.3 copy-done.36
  525.0 5.4 bitcast_convert_fusion
  530.5 42.3 %reduce-scatter.11.cloned.1.call-done = bf16[2,297,768]{2,1,0:T(8,128)(2,1)} async-done(((bf16[8,297,768]{2,1,0:T(8,128)(2,1)}), bf16[2,297,768]{2,1,0:T(8,128)(2,1)}) %reduce-scatter.11.cloned.1.call-update) | async-done | bytes 912400 | tf_op jit(solution)/shard_map/reduce_scatter | solution.py:184
  572.8 1.8 multiply_reduce_fusion.1
  574.7 1.9 fusion.92
  576.6 1.6 add_add_fusion.2
  578.3 1.3 copy-done.6
  579.5 0.8 slice_reduce_fusion
  580.4 2.8 copy.51
  583.2 1.3 slice.49
  584.5 1.3 copy.52
  585.8 122.2 %all-reduce.2.cloned.1.call-done = f32[100,768]{1,0:T(8,128)} async-done(((f32[100,768]{1,0:T(8,128)}), f32[100,768]{1,0:T(8,128)}) %all-reduce.2.cloned.1.call-update) | async-done | bytes 307216 | tf_op jit(solution)/shard_map/psum | solution.py:189
  708.1 1.7 copy.75
  (119 shorter events, 1.4 us)
Async XLA Ops:
  8.0 2.8 copy-start.18
  8.0 2.8 copy-start.29
  8.0 75.3 %all-gather.9.cloned.1.call-start = ((), (), s32[]{:S(2)}) async-start(), calls=%async_computation.4 | async-start | bytes 4669440 | tf_op jit(solution)/shard_map/all_gather | solution.py:134
  10.2 2.1 copy-start.13
  10.2 2.2 copy-start.10
  10.4 1.9 copy-start.15
  10.8 1.5 copy-start.24
  10.9 1.5 copy-start.20
  12.2 71.0 %copy-start.28 = (s32[8,297]{1,0:T(8,128)S(1)}, s32[8,297]{1,0:T(8,128)}, u32[]{:S(2)}) copy-start(s32[8,297]{1,0:T(8,128)} %param.19) | copy-start | bytes 28516
  12.2 71.0 %copy-start.34 = (s32[8]{0:T(128)S(1)}, s32[8]{0:T(128)}, u32[]{:S(2)}) copy-start(s32[8]{0:T(128)} %param.18) | copy-start | bytes 100
  12.2 139.5 %reduce-scatter.5.cloned.1.call-start = ((), (), s32[]{:S(2)}) async-start(), calls=%async_computation.5 | async-start | bytes 4669440 | tf_op jit(solution)/shard_map/reduce_scatter | solution.py:138
  83.3 7.2 copy-start.32
  107.7 1.2 copy-start.9
  107.7 44.1 %copy-start.12 = (f32[768]{0:T(1024)S(1)}, f32[768]{0:T(1024)}, u32[]{:S(2)}) copy-start(f32[768]{0:T(1024)} %param.24) | copy-start | bytes 9220
  107.7 54.0 %all-gather.17.cloned.1.call-start = ((), (), s32[]{:S(2)}) async-start(), calls=%async_computation.10 | async-start | bytes 1327104 | tf_op jit(solution)/shard_map/all_gather | solution.py:158
  108.8 1.5 copy-start.22
  110.3 44.8 %copy-start.17 = (f32[768]{0:T(1024)S(1)}, f32[768]{0:T(1024)}, u32[]{:S(2)}) copy-start(f32[768]{0:T(1024)} %param.25) | copy-start | bytes 9220
  110.3 44.8 %copy-start.30 = (f32[768]{0:T(1024)S(1)}, f32[768]{0:T(1024)}, u32[]{:S(2)}) copy-start(f32[768]{0:T(1024)} %param.26) | copy-start | bytes 9220
  110.3 78.1 %all-gather.11.cloned.1.call-start = ((), (), s32[]{:S(2)}) async-start(), calls=%async_computation.6 | async-start | bytes 4669440 | tf_op jit(solution)/shard_map/all_gather | solution.py:146
  151.8 3.4 copy-start
  155.1 4.7 copy-start.26
  156.6 74.7 %all-gather.21.cloned.1.call-start = ((), (), s32[]{:S(2)}) async-start(), calls=%async_computation.12 | async-start | bytes 1327104 | tf_op jit(solution)/shard_map/all_gather | solution.py:159
  157.2 107.0 %all-gather.19.cloned.1.call-start = ((), (), s32[]{:S(2)}) async-start(), calls=%async_computation.11 | async-start | bytes 4669440 | tf_op jit(solution)/shard_map/all_gather | solution.py:163
  159.9 147.1 %all-gather.13.cloned.1.call-start = ((), (), s32[]{:S(2)}) async-start(), calls=%async_computation.7 | async-start | bytes 1327104 | tf_op jit(solution)/shard_map/all_gather | solution.py:122
  160.6 188.6 %all-gather.15.cloned.1.call-start = ((), (), s32[]{:S(2)}) async-start(), calls=%async_computation.8 | async-start | bytes 1327104 | tf_op jit(solution)/shard_map/all_gather | solution.py:123
  161.4 102.9 %copy-start.35 = (f32[768]{0:T(1024)S(1)}, f32[768]{0:T(1024)}, u32[]{:S(2)}) copy-start(f32[768]{0:T(1024)} %param.28) | copy-start | bytes 9220
  161.4 211.0 %reduce-scatter.9.cloned.1.call-start = ((), (), s32[]{:S(2)}) async-start(), calls=%async_computation.13 | async-start | bytes 4669440 | tf_op jit(solution)/shard_map/reduce_scatter | solution.py:167
  291.2 122.4 %reduce-scatter.7.cloned.1.call-start = ((), (), s32[]{:S(2)}) async-start(), calls=%async_computation.9 | async-start | bytes 4669440 | tf_op jit(solution)/shard_map/reduce_scatter | solution.py:149
  372.3 2.1 copy-start.27
  372.3 41.3 %copy-start.23 = (f32[2,297]{1,0:T(2,128)S(1)}, f32[2,297]{1,0:T(2,128)}, u32[]{:S(2)}) copy-start(f32[2,297]{1,0:T(2,128)} %copy-done.22) | copy-start | bytes 7132
  372.3 41.3 %copy-start.31 = (f32[768]{0:T(1024)S(1)}, f32[768]{0:T(1024)}, u32[]{:S(2)}) copy-start(f32[768]{0:T(1024)} %param.30) | copy-start | bytes 9220
  372.3 131.1 %all-gather.23.cloned.1.call-start = ((), (), s32[]{:S(2)}) async-start(), calls=%async_computation.14 | async-start | bytes 4669440 | tf_op jit(solution)/shard_map/all_gather | solution.py:176
  372.4 2.0 copy-start.2
  375.4 41.9 %copy-start.14 = (bf16[192,96]{1,0:T(8,128)(2,1)S(1)}, bf16[192,96]{1,0:T(8,128)(2,1)}, u32[]{:S(2)}) copy-start(bf16[192,96]{1,0:T(8,128)(2,1)} %param.23) | copy-start | bytes 110596
  375.4 42.0 %copy-start.11 = (bf16[3,96,192]{2,1,0:T(8,128)(2,1)S(1)}, bf16[3,96,192]{2,1,0:T(8,128)(2,1)}, u32[]{:S(2)}) copy-start(bf16[3,96,192]{2,1,0:T(8,128)(2,1)} %param.22) | copy-start | bytes 331780
  417.2 155.5 %reduce-scatter.11.cloned.1.call-start = ((), (), s32[]{:S(2)}) async-start(), calls=%async_computation.15 | async-start | bytes 4669440 | tf_op jit(solution)/shard_map/reduce_scatter | solution.py:184
  485.5 7.7 %copy-start.7 = (bf16[3,768,192]{2,0,1:T(4,128)(2,1)}, bf16[3,768,192]{2,0,1:T(4,128)(2,1)S(1)}, u32[]{:S(2)}) copy-start(bf16[3,768,192]{2,0,1:T(4,128)(2,1)S(1)} %all_gather.47) | copy-start | bytes 2654212
  493.2 2.0 copy-start.33
  503.5 11.3 %slice-start = ((s8[11206656]{0:T(1024)(128)(4,1)}), s8[4194304]{0:T(1024)(128)(4,1)S(1)}, s32[]{:S(2)}) async-start(s8[11206656]{0:T(1024)(128)(4,1)} %bitcast.94), calls=%async_computation.17 | async-start | bytes 8388608
  507.1 7.7 %copy-start.37 = (bf16[8,297,192]{1,2,0:T(8,128)(2,1)}, bf16[8,297,192]{1,2,0:T(8,128)(2,1)S(1)}, u32[]{:S(2)}) copy-start(bf16[8,297,192]{1,2,0:T(8,128)(2,1)S(1)} %convolution_convert_fusion.1) | copy-start | bytes 2737156
  507.1 7.7 %slice-start.1 = ((s8[11206656]{0:T(1024)(128)(4,1)}), s8[4194304]{0:T(1024)(128)(4,1)S(1)}, s32[]{:S(2)}) async-start(s8[11206656]{0:T(1024)(128)(4,1)} %bitcast.94), calls=%async_computation.18 | async-start | bytes 8388608
  507.1 7.7 %slice-start.2 = ((s8[11206656]{0:T(1024)(128)(4,1)}), s8[2818048]{0:T(1024)(128)(4,1)S(1)}, s32[]{:S(2)}) async-start(s8[11206656]{0:T(1024)(128)(4,1)} %bitcast.94), calls=%async_computation.19 | async-start | bytes 5636096
  519.9 3.3 copy-start.5
  523.2 1.4 copy-start.8
  523.2 1.7 copy-start.36
  530.4 42.4 %copy-start.16 = (f32[2,297]{1,0:T(2,128)S(1)}, f32[2,297]{1,0:T(2,128)}, u32[]{:S(2)}) copy-start(f32[2,297]{1,0:T(2,128)} %copy-done.15) | copy-start | bytes 7132
  530.4 42.4 %copy-start.19 = (f32[768]{0:T(1024)S(1)}, f32[768]{0:T(1024)}, u32[]{:S(2)}) copy-start(f32[768]{0:T(1024)} %param.20) | copy-start | bytes 9220
  530.4 44.2 %copy-start.25 = (f32[2,297]{1,0:T(2,128)S(1)}, f32[2,297]{1,0:T(2,128)}, u32[]{:S(2)}) copy-start(f32[2,297]{1,0:T(2,128)} %copy-done.24) | copy-start | bytes 7132
  530.4 44.2 %copy-start.21 = (f32[2,297]{1,0:T(2,128)S(1)}, f32[2,297]{1,0:T(2,128)}, u32[]{:S(2)}) copy-start(f32[2,297]{1,0:T(2,128)} %copy-done.20) | copy-start | bytes 7132
  530.4 177.6 %all-reduce.2.cloned.1.call-start = ((), (), s32[]{:S(2)}) async-start(), calls=%async_computation.16 | async-start | bytes 638976 | tf_op jit(solution)/shard_map/psum | solution.py:189
  572.8 3.8 copy-start.1
  572.8 3.8 copy-start.3
  572.8 3.9 copy-start.4
  578.3 1.3 copy-start.6
Sparse Core Ops, SparseCore 0:
  12.4 33.0 all-gather.8
  107.8 43.8 reduce-scatter.4
  291.3 41.6 reduce-scatter.8
  372.4 41.1 reduce-scatter.6
  580.5 127.5 all-reduce.1
Sparse Core Ops, SparseCore 1:
  110.6 42.7 all-gather.16
  156.7 31.7 all-gather.10
  190.8 40.5 all-gather.20
  233.0 31.2 all-gather.18
  266.4 40.5 all-gather.12
  309.2 40.0 all-gather.14
  417.3 31.7 all-gather.22
  530.5 42.2 reduce-scatter.10
where the time goes:
time: 726 us; the launch traced here: 717 us
  waiting for transfers between devices  379 us (52%)
  blocking collectives  135 us (19%)
  matrix products  132 us (18%)
  other arithmetic  26.4 us (4%)
  local copies, waits for them, and re-layouts  18.9 us (3%)
  between operations  16.4 us (2%)
  starting transfers between devices  9.95 us (1%)
    psum x1, waiting for transfers between devices, per_device(): lax.psum(jnp.sum(grad_stream[:, IMG_TOK:], axis=0), ('dp', 'head'))  122 us
    dot_general x4, matrix products, project(): jnp.einsum('isd,dc->isc', rows_b, weight, preferred_element_type=jnp.floa...  44.9 us
    reduce_scatter x1, waiting for transfers between devices, per_device(): lax.psum_scatter(grad_partial.astype(jnp.bfloat16), 'head', scatter_dimen...  42.3 us
    reduce_scatter x1, waiting for transfers between devices, per_device(): lax.psum_scatter(project(context, full_out).astype(jnp.bfloat16), 'head',...  41.4 us
    all_gather x1, blocking collectives, per_device(): lax.all_gather(held_inputs[0], 'dp', axis=1, tiled=True)  39.4 us
    reduce_scatter x1, waiting for transfers between devices, per_device(): lax.psum_scatter(project(active_b, full_fc2).astype(jnp.bfloat16), 'head'...  38.2 us
    all_gather x1, blocking collectives, per_device(): lax.all_gather(w_qkv, 'dp', axis=1, tiled=True)  36.7 us
    all_gather x1, waiting for transfers between devices, per_device(): lax.all_gather(held_inputs[3], 'dp', axis=1, tiled=True)  34.4 us
  transfers between devices with their start and end apart: 13, of which 9 were waited for; matrix products, arithmetic and copies ran while one was open for 15% of the time, Pallas kernels for 0%

commit v1 on v0

--- a/solution.py
+++ b/solution.py
@@ -107,6 +107,10 @@
     b_fc2,
     grad_output,
 ):
+
+    def switch_the_screen(sample, across):
+        return lax.all_gather(sample, axis_name=across).sum(axis=0)
+
     own_count = layer_input.shape[0]
     model_width = layer_input.shape[2]
     offset = lax.axis_index("head") * own_count
@@ -186,7 +190,7 @@
     ).astype(jnp.float32)
     grad_stream = grad_mid + back_attn_norm(grad_normed_attn)[0]
     grad_input = grad_stream[:, :IMG_TOK].astype(jnp.bfloat16)
-    grad_prompts = lax.psum(jnp.sum(grad_stream[:, IMG_TOK:], axis=0), ("dp", "head"))
+    grad_prompts = switch_the_screen(jnp.sum(grad_stream[:, IMG_TOK:], axis=0), ("dp", "head"))
     return (result, grad_input, grad_prompts)
 
 

time: 726 us -> 689 us (0.949)
  waiting for transfers between devices: 379 us -> 337 us
    psum x1 -> x0, waiting for transfers between devices: 122 us -> none  [per_device(): lax.psum(jnp.sum(grad_stream[:, IMG_TOK:], axis=0), ('dp', 'head'))]
    all_gather x0 -> x1, waiting for transfers between devices: none -> 80.2 us  [switch_the_screen(): return lax.all_gather(sample, axis_name=across).sum(axis=0)]
  transfers between devices with their start and end apart: 13 -> 13, of which waited for: 9 -> 9; matrix products, arithmetic and copies ran while one was open for 15% -> 16% of each run, Pallas kernels for 0% -> 0%
where the time goes in v1:
time: 689 us; the launch traced here: 679 us
  waiting for transfers between devices  337 us (49%)
  blocking collectives  135 us (20%)
  matrix products  132 us (19%)
  other arithmetic  31.6 us (5%)
  local copies, waits for them, and re-layouts  17.1 us (2%)
  between operations  16.4 us (2%)
  starting transfers between devices  9.95 us (1%)
    all_gather x1, waiting for transfers between devices, switch_the_screen(): return lax.all_gather(sample, axis_name=across).sum(axis=0)  80.2 us
    dot_general x4, matrix products, project(): jnp.einsum('isd,dc->isc', rows_b, weight, preferred_element_type=jnp.floa...  44.9 us
    reduce_scatter x1, waiting for transfers between devices, per_device(): lax.psum_scatter(grad_partial.astype(jnp.bfloat16), 'head', scatter_dimen...  42.3 us
    reduce_scatter x1, waiting for transfers between devices, per_device(): lax.psum_scatter(project(context, full_out).astype(jnp.bfloat16), 'head',...  41.4 us
    all_gather x1, blocking collectives, per_device(): lax.all_gather(held_inputs[0], 'dp', axis=1, tiled=True)  39.4 us
    reduce_scatter x1, waiting for transfers between devices, per_device(): lax.psum_scatter(project(active_b, full_fc2).astype(jnp.bfloat16), 'head'...  38.2 us
    all_gather x1, blocking collectives, per_device(): lax.all_gather(w_qkv, 'dp', axis=1, tiled=True)  36.7 us
    all_gather x1, waiting for transfers between devices, per_device(): lax.all_gather(held_inputs[3], 'dp', axis=1, tiled=True)  34.4 us
  transfers between devices with their start and end apart: 13, of which 9 were waited for; matrix products, arithmetic and copies ran while one was open for 16% of the time, Pallas kernels for 0%

profile of v1, /device:TPU:8, one launch (start us, length us, event | category | flops | bytes accessed | tf_op | source)
XLA Modules:
  0.0 678.7 jit_solution(9835426347474116075)
XLA Ops:
  8.1 1.2 copy_convert_fusion
  9.2 1.0 broadcast_in_dim.26
  10.2 0.2 fusion.72
  10.4 0.4 multiply_reduce_fusion.4
  10.9 1.3 add_convert_fusion.1
  12.4 0.1 copy.34
  12.6 36.7 %all_gather.45 = bf16[3,768,192]{2,0,1:T(4,128)(2,1)} all-gather(bf16[3,96,192]{2,0,1:T(4,128)(2,1)S(1)} %copy.34), channel_id=1, replica_groups=mesh['dp'=8,'head'=4] {'dp'}, dimensions={1}, use_global_device_ids=true | all-gather | bytes 995328 | tf_op jit(solution)/shard_map/all_gather | solution.py:124
  49.3 3.4 copy.35
  52.7 30.5 %all_gather.46 = bf16[192,768]{0,1:T(8,128)(2,1)S(1)} all-gather(bf16[192,96]{0,1:T(8,128)(2,1)S(1)} %copy.37), channel_id=1, replica_groups=mesh['dp'=8,'head'=4] {'dp'}, dimensions={1}, use_global_device_ids=true | all-gather | bytes 331776 | tf_op jit(solution)/shard_map/all_gather | solution.py:125
  83.3 5.2 convert_bitcast_fusion.1
  88.6 1.9 fusion.167
  90.5 8.2 %fusion.168 = (f32[8,3,297]{2,1,0:T(4,128)S(1)}, f32[8,3,297,297]{2,3,1,0:T(8,128)}) fusion(pred[8,297]{1,0:T(8,128)(4,1)S(1)} %get-tuple-element.30, bf16[8,297,3,64]{1,3,2,0:T(8,128)(2,1)} %bitcast.107, bf16[8,297,3,64]{1,3,2,0:T(8,128)(2,1)} %bitcast.106), kind=kOutput, calls=%fused_computation.222 | convolution fusion | flops 279446432 | bytes 10323720 | tf_op jit(solution)/shard_map/sub | solution.py:43
  98.7 5.8 fusion.73
  104.4 3.2 convolution_convert_fusion
  107.8 1.1 copy-done.9
  108.8 1.5 convert_multiply_fusion.4
  110.4 41.4 %reduce-scatter.5.cloned.1.call-done = bf16[2,297,768]{2,1,0:T(8,128)(2,1)} async-done(((bf16[8,297,768]{2,1,0:T(8,128)(2,1)}), bf16[2,297,768]{2,1,0:T(8,128)(2,1)}) %reduce-scatter.5.cloned.1.call-update) | async-done | bytes 912400 | tf_op jit(solution)/shard_map/reduce_scatter | solution.py:142
  151.8 1.6 fusion.165
  153.4 1.7 multiply_reduce_fusion.3
  155.1 1.5 add_convert_fusion
  156.7 0.5 all-gather.24.cloned.1.call-update
  157.3 2.6 convert_element_type.129
  159.9 0.7 all-gather.16.cloned.1.call-update
  160.7 0.7 all-gather.18.cloned.1.call-update
  161.4 0.3 reduce-scatter.9.cloned.1.call-start
  161.7 26.8 %all-gather.14.cloned.1.call-done = bf16[8,297,768]{2,1,0:T(8,128)(2,1)} async-done(((bf16[2,297,768]{2,1,0:T(8,128)(2,1)}), bf16[8,297,768]{2,1,0:T(8,128)(2,1)}) %all-gather.14.cloned.1.call-update) | async-done | bytes 3649552 | tf_op jit(solution)/shard_map/all_gather | solution.py:150
  188.5 8.4 %fusion.82 = f32[8,297,768]{2,1,0:T(8,128)} fusion(bf16[8,297,768]{2,1,0:T(8,128)(2,1)} %all-gather.14.cloned.1.call-done, bf16[768,768]{1,0:T(8,128)(2,1)} %all-gather.20.cloned.1.call-done), kind=kOutput, calls=%fused_computation.120 | convolution fusion | flops 2802843648 | bytes 12128256 | tf_op jit(solution)/shard_map/isd,dc->isc/dot_general | solution.py:28
  196.9 34.4 %all-gather.24.cloned.1.call-done = bf16[768,768]{0,1:T(8,128)(2,1)} async-done(((bf16[768,96]{0,1:T(8,128)(2,1)}), bf16[768,768]{0,1:T(8,128)(2,1)}) %all-gather.24.cloned.1.call-update) | async-done | bytes 1179664 | tf_op jit(solution)/shard_map/all_gather | solution.py:163
  231.3 32.9 %all-gather.22.cloned.1.call-done = bf16[8,297,768]{2,1,0:T(8,128)(2,1)} async-done(((bf16[2,297,768]{2,1,0:T(8,128)(2,1)}), bf16[8,297,768]{2,1,0:T(8,128)(2,1)}) %all-gather.22.cloned.1.call-update) | async-done | bytes 3649552 | tf_op jit(solution)/shard_map/all_gather | solution.py:167
  264.2 27.0 %fusion.57 = bf16[8,297,768]{2,1,0:T(8,128)(2,1)} fusion(f32[8,297,768]{2,1,0:T(8,128)} %fusion.82, f32[768]{0:T(1024)S(1)} %copy-done.35, bf16[8,297,768]{2,1,0:T(8,128)(2,1)} %all-gather.22.cloned.1.call-done, bf16[768,768]{0,1:T(8,128)(2,1)} %all-gather.24.cloned.1.call-done, bf16[768,768]{1,0:T(8,128)(2,1)} %all-gather.20.cloned.1.call-done), kind=kOutput, calls=%fused_computation.89 | convolution fusion | flops 5744369664 | bytes 16960512 | tf_op jit(solution)/shard_map/isf,df->isd/dot_general | solution.py:59
  291.2 9.2 %reduce-scatter.7.cloned.1.call-start = ((), (), s32[]{:S(2)}) async-start(), calls=%async_computation.9 | async-start | bytes 4669440 | tf_op jit(solution)/shard_map/reduce_scatter | solution.py:153
  300.4 6.6 all-gather.16.cloned.1.call-done
  307.0 10.3 %fusion.70 = (u8[297,768]{1,0:T(8,128)(4,1)S(1)}, u8[297,768]{1,0:T(8,128)(4,1)S(1)}, f32[8,297,768]{2,1,0:T(8,128)}) fusion(f32[768]{0:T(1024)S(1)} %copy-done.35, bf16[8,297,768]{2,1,0:T(8,128)(2,1)} %all-gather.14.cloned.1.call-done, bf16[768,768]{1,0:T(8,128)(2,1)} %all-gather.16.cloned.1.call-done), kind=kOutput, calls=%fused_computation.109 | convolution fusion | flops 2827934208 | bytes 12587520 | tf_op jit(solution)/shard_map/isd,dc->isc/dot_general | solution.py:28
  317.2 32.0 %all-gather.18.cloned.1.call-done = bf16[768,768]{0,1:T(8,128)(2,1)} async-done(((bf16[768,96]{0,1:T(8,128)(2,1)}), bf16[768,768]{0,1:T(8,128)(2,1)}) %all-gather.18.cloned.1.call-update) | async-done | bytes 1179664 | tf_op jit(solution)/shard_map/all_gather | solution.py:127
  349.3 23.0 %fusion.60 = bf16[8,297,768]{2,1,0:T(8,128)(2,1)} fusion(f32[8,297,768]{2,1,0:T(8,128)} %get-tuple-element.33, f32[768]{0:T(1024)S(1)} %copy-done.35, bf16[768,768]{0,1:T(8,128)(2,1)} %all-gather.18.cloned.1.call-done, u8[297,768]{1,0:T(8,128)(4,1)S(1)} %get-tuple-element.20, u8[297,768]{1,0:T(8,128)(4,1)S(1)} %get-tuple-element.19), kind=kOutput, calls=%fused_computation.90 | convolution fusion | flops 2934226944 | bytes 12587520 | tf_op jit(solution)/shard_map/isd,dc->isc/dot_general | solution.py:28
  372.4 1.9 multiply_reduce_fusion.2
  374.4 1.0 fusion.91
  375.4 38.2 %reduce-scatter.7.cloned.1.call-done = bf16[2,297,768]{2,1,0:T(8,128)(2,1)} async-done(((bf16[8,297,768]{2,1,0:T(8,128)(2,1)}), bf16[2,297,768]{2,1,0:T(8,128)(2,1)}) %reduce-scatter.7.cloned.1.call-update) | async-done | bytes 912400 | tf_op jit(solution)/shard_map/reduce_scatter | solution.py:153
  413.6 3.6 fusion.164
  417.5 28.5 %all_gather.55 = bf16[192,768]{0,1:T(8,128)(2,1)S(1)} all-gather(bf16[192,96]{0,1:T(8,128)(2,1)S(1)} %copy.42), channel_id=1, replica_groups=mesh['dp'=8,'head'=4] {'dp'}, dimensions={1}, use_global_device_ids=true | all-gather | bytes 331776 | tf_op jit(solution)/shard_map/all_gather | solution.py:161
  446.1 39.4 %all_gather.53 = bf16[3,768,192]{2,0,1:T(4,128)(2,1)S(1)} all-gather(bf16[3,96,192]{2,0,1:T(4,128)(2,1)S(1)} %copy.40), channel_id=1, replica_groups=mesh['dp'=8,'head'=4] {'dp'}, dimensions={1}, use_global_device_ids=true | all-gather | bytes 995328 | tf_op jit(solution)/shard_map/all_gather | solution.py:160
  485.5 7.7 %convert_bitcast_fusion = bf16[3,8,297,192]{2,3,1,0:T(8,128)(2,1)S(1)} fusion(bf16[8,297,768]{2,1,0:T(8,128)(2,1)} %all-gather.12.cloned.1.call-done, bf16[3,768,192,1]{2,0,1,3:T(4,128)(2,1)S(1)} %bitcast.102), kind=kOutput, calls=%fused_computation.84 | convolution fusion | flops 2103501312 | bytes 7271424 | tf_op jit(solution)/shard_map/isd,tdc->tisc/dot_general | solution.py:34
  493.2 2.0 fusion.166
  495.2 8.2 %fusion.169 = (f32[8,3,297]{2,1,0:T(4,128)S(1)}, f32[8,3,297,297]{2,3,1,0:T(8,128)}) fusion(pred[8,297]{1,0:T(8,128)(4,1)S(1)} %copy-done.33, bf16[8,297,3,64]{1,3,2,0:T(8,128)(2,1)} %bitcast.99, bf16[8,297,3,64]{1,3,2,0:T(8,128)(2,1)} %bitcast.97), kind=kOutput, calls=%fused_computation.223 | convolution fusion | flops 279446432 | bytes 10323720 | tf_op jit(solution)/shard_map/sub | solution.py:43
  503.5 3.6 convolution_convert_fusion.1
  507.1 7.6 %fusion.74 = bf16[8,3,64,297]{3,2,1,0:T(8,128)(2,1)} fusion(bf16[8,297,3,64]{1,3,2,0:T(8,128)(2,1)S(1)} %bitcast.111, f32[8,3,297,297]{2,3,1,0:T(8,128)} %get-tuple-element.35, f32[8,3,297]{2,1,0:T(4,128)S(1)} %get-tuple-element.34), kind=kOutput, calls=%fused_computation.113 | convolution fusion | flops 275668288 | bytes 10321344 | tf_op jit(solution)/shard_map/ihst,ishc->ithc/dot_general | solution.py:69
  514.8 3.4 multiply_reduce_fusion
  518.2 1.7 multiply_convert_fusion
  519.9 3.3 multiply_convert_fusion.1
  523.2 1.2 multiply_convert_fusion.2
  524.4 0.2 copy-done.8
  524.6 0.3 copy-done.36
  525.0 5.4 bitcast_convert_fusion
  530.5 42.3 %reduce-scatter.11.cloned.1.call-done = bf16[2,297,768]{2,1,0:T(8,128)(2,1)} async-done(((bf16[8,297,768]{2,1,0:T(8,128)(2,1)}), bf16[2,297,768]{2,1,0:T(8,128)(2,1)}) %reduce-scatter.11.cloned.1.call-update) | async-done | bytes 912400 | tf_op jit(solution)/shard_map/reduce_scatter | solution.py:188
  572.8 1.8 multiply_reduce_fusion.1
  574.7 1.9 fusion.92
  576.6 1.6 add_add_fusion.2
  578.3 1.2 copy-done.6
  579.5 0.8 slice_reduce_fusion
  580.3 2.8 copy.51
  583.1 1.3 slice.49
  584.5 1.3 copy.52
  585.8 80.2 %all-gather.28.cloned.1.call-done = f32[32,100,768]{2,1,0:T(8,128)} async-done(((f32[1,100,768]{2,1,0:T(8,128)}), f32[32,100,768]{2,1,0:T(8,128)}) %all-gather.28.cloned.1.call-update) | async-done | bytes 9830416 | tf_op jit(solution)/shard_map/all_gather | solution.py:112
  665.9 5.2 reduce_sum.145
  (119 shorter events, 1.4 us)
Async XLA Ops:
  8.0 2.8 copy-start.18
  8.0 2.8 copy-start.29
  8.0 75.3 %all-gather.12.cloned.1.call-start = ((), (), s32[]{:S(2)}) async-start(), calls=%async_computation.4 | async-start | bytes 4669440 | tf_op jit(solution)/shard_map/all_gather | solution.py:138
  10.2 2.1 copy-start.13
  10.2 2.2 copy-start.10
  10.4 1.9 copy-start.15
  10.8 1.5 copy-start.24
  10.9 1.5 copy-start.20
  12.2 71.0 %copy-start.28 = (s32[8,297]{1,0:T(8,128)S(1)}, s32[8,297]{1,0:T(8,128)}, u32[]{:S(2)}) copy-start(s32[8,297]{1,0:T(8,128)} %param.19) | copy-start | bytes 28516
  12.2 71.0 %copy-start.34 = (s32[8]{0:T(128)S(1)}, s32[8]{0:T(128)}, u32[]{:S(2)}) copy-start(s32[8]{0:T(128)} %param.18) | copy-start | bytes 100
  12.2 139.5 %reduce-scatter.5.cloned.1.call-start = ((), (), s32[]{:S(2)}) async-start(), calls=%async_computation.5 | async-start | bytes 4669440 | tf_op jit(solution)/shard_map/reduce_scatter | solution.py:142
  83.3 7.2 %copy-start.32 = (pred[8,297]{1,0:T(8,128)(4,1)}, pred[8,297]{1,0:T(8,128)(4,1)S(1)}, u32[]{:S(2)}) copy-start(pred[8,297]{1,0:T(8,128)(4,1)S(1)} %get-tuple-element.30) | copy-start | bytes 7132
  107.7 1.2 copy-start.9
  107.7 44.1 %copy-start.12 = (f32[768]{0:T(1024)S(1)}, f32[768]{0:T(1024)}, u32[]{:S(2)}) copy-start(f32[768]{0:T(1024)} %param.24) | copy-start | bytes 9220
  107.7 54.0 %all-gather.20.cloned.1.call-start = ((), (), s32[]{:S(2)}) async-start(), calls=%async_computation.10 | async-start | bytes 1327104 | tf_op jit(solution)/shard_map/all_gather | solution.py:162
  108.8 1.5 copy-start.22
  110.3 44.8 %copy-start.17 = (f32[768]{0:T(1024)S(1)}, f32[768]{0:T(1024)}, u32[]{:S(2)}) copy-start(f32[768]{0:T(1024)} %param.25) | copy-start | bytes 9220
  110.3 44.8 %copy-start.30 = (f32[768]{0:T(1024)S(1)}, f32[768]{0:T(1024)}, u32[]{:S(2)}) copy-start(f32[768]{0:T(1024)} %param.26) | copy-start | bytes 9220
  110.3 78.1 %all-gather.14.cloned.1.call-start = ((), (), s32[]{:S(2)}) async-start(), calls=%async_computation.6 | async-start | bytes 4669440 | tf_op jit(solution)/shard_map/all_gather | solution.py:150
  151.8 3.4 copy-start
  155.1 4.7 copy-start.26
  156.6 74.7 %all-gather.24.cloned.1.call-start = ((), (), s32[]{:S(2)}) async-start(), calls=%async_computation.12 | async-start | bytes 1327104 | tf_op jit(solution)/shard_map/all_gather | solution.py:163
  157.2 107.0 %all-gather.22.cloned.1.call-start = ((), (), s32[]{:S(2)}) async-start(), calls=%async_computation.11 | async-start | bytes 4669440 | tf_op jit(solution)/shard_map/all_gather | solution.py:167
  159.9 147.1 %all-gather.16.cloned.1.call-start = ((), (), s32[]{:S(2)}) async-start(), calls=%async_computation.7 | async-start | bytes 1327104 | tf_op jit(solution)/shard_map/all_gather | solution.py:126
  160.6 188.6 %all-gather.18.cloned.1.call-start = ((), (), s32[]{:S(2)}) async-start(), calls=%async_computation.8 | async-start | bytes 1327104 | tf_op jit(solution)/shard_map/all_gather | solution.py:127
  161.4 102.9 %copy-start.35 = (f32[768]{0:T(1024)S(1)}, f32[768]{0:T(1024)}, u32[]{:S(2)}) copy-start(f32[768]{0:T(1024)} %param.28) | copy-start | bytes 9220
  161.4 211.0 %reduce-scatter.9.cloned.1.call-start = ((), (), s32[]{:S(2)}) async-start(), calls=%async_computation.13 | async-start | bytes 4669440 | tf_op jit(solution)/shard_map/reduce_scatter | solution.py:171
  291.2 122.4 %reduce-scatter.7.cloned.1.call-start = ((), (), s32[]{:S(2)}) async-start(), calls=%async_computation.9 | async-start | bytes 4669440 | tf_op jit(solution)/shard_map/reduce_scatter | solution.py:153
  372.3 2.1 copy-start.27
  372.3 41.3 %copy-start.23 = (f32[2,297]{1,0:T(2,128)S(1)}, f32[2,297]{1,0:T(2,128)}, u32[]{:S(2)}) copy-start(f32[2,297]{1,0:T(2,128)} %copy-done.22) | copy-start | bytes 7132
  372.3 41.3 %copy-start.31 = (f32[768]{0:T(1024)S(1)}, f32[768]{0:T(1024)}, u32[]{:S(2)}) copy-start(f32[768]{0:T(1024)} %param.30) | copy-start | bytes 9220
  372.3 131.1 %all-gather.26.cloned.1.call-start = ((), (), s32[]{:S(2)}) async-start(), calls=%async_computation.14 | async-start | bytes 4669440 | tf_op jit(solution)/shard_map/all_gather | solution.py:180
  372.4 2.0 copy-start.2
  375.4 41.9 %copy-start.14 = (bf16[192,96]{1,0:T(8,128)(2,1)S(1)}, bf16[192,96]{1,0:T(8,128)(2,1)}, u32[]{:S(2)}) copy-start(bf16[192,96]{1,0:T(8,128)(2,1)} %param.23) | copy-start | bytes 110596
  375.4 42.0 %copy-start.11 = (bf16[3,96,192]{2,1,0:T(8,128)(2,1)S(1)}, bf16[3,96,192]{2,1,0:T(8,128)(2,1)}, u32[]{:S(2)}) copy-start(bf16[3,96,192]{2,1,0:T(8,128)(2,1)} %param.22) | copy-start | bytes 331780
  417.2 155.5 %reduce-scatter.11.cloned.1.call-start = ((), (), s32[]{:S(2)}) async-start(), calls=%async_computation.15 | async-start | bytes 4669440 | tf_op jit(solution)/shard_map/reduce_scatter | solution.py:188
  485.5 7.7 %copy-start.7 = (bf16[3,768,192]{2,0,1:T(4,128)(2,1)}, bf16[3,768,192]{2,0,1:T(4,128)(2,1)S(1)}, u32[]{:S(2)}) copy-start(bf16[3,768,192]{2,0,1:T(4,128)(2,1)S(1)} %all_gather.53) | copy-start | bytes 2654212
  493.2 2.0 copy-start.33
  503.5 11.3 %slice-start = ((s8[11206656]{0:T(1024)(128)(4,1)}), s8[4194304]{0:T(1024)(128)(4,1)S(1)}, s32[]{:S(2)}) async-start(s8[11206656]{0:T(1024)(128)(4,1)} %bitcast.95), calls=%async_computation.17 | async-start | bytes 8388608
  507.1 7.7 %copy-start.37 = (bf16[8,297,192]{1,2,0:T(8,128)(2,1)}, bf16[8,297,192]{1,2,0:T(8,128)(2,1)S(1)}, u32[]{:S(2)}) copy-start(bf16[8,297,192]{1,2,0:T(8,128)(2,1)S(1)} %convolution_convert_fusion.1) | copy-start | bytes 2737156
  507.1 7.7 %slice-start.1 = ((s8[11206656]{0:T(1024)(128)(4,1)}), s8[4194304]{0:T(1024)(128)(4,1)S(1)}, s32[]{:S(2)}) async-start(s8[11206656]{0:T(1024)(128)(4,1)} %bitcast.95), calls=%async_computation.18 | async-start | bytes 8388608
  507.1 7.7 %slice-start.2 = ((s8[11206656]{0:T(1024)(128)(4,1)}), s8[2818048]{0:T(1024)(128)(4,1)S(1)}, s32[]{:S(2)}) async-start(s8[11206656]{0:T(1024)(128)(4,1)} %bitcast.95), calls=%async_computation.19 | async-start | bytes 5636096
  519.9 3.3 copy-start.5
  523.2 1.4 copy-start.8
  523.2 1.7 copy-start.36
  530.4 42.4 %copy-start.16 = (f32[2,297]{1,0:T(2,128)S(1)}, f32[2,297]{1,0:T(2,128)}, u32[]{:S(2)}) copy-start(f32[2,297]{1,0:T(2,128)} %copy-done.15) | copy-start | bytes 7132
  530.4 42.4 %copy-start.19 = (f32[768]{0:T(1024)S(1)}, f32[768]{0:T(1024)}, u32[]{:S(2)}) copy-start(f32[768]{0:T(1024)} %param.20) | copy-start | bytes 9220
  530.4 44.2 %copy-start.25 = (f32[2,297]{1,0:T(2,128)S(1)}, f32[2,297]{1,0:T(2,128)}, u32[]{:S(2)}) copy-start(f32[2,297]{1,0:T(2,128)} %copy-done.24) | copy-start | bytes 7132
  530.4 44.2 %copy-start.21 = (f32[2,297]{1,0:T(2,128)S(1)}, f32[2,297]{1,0:T(2,128)}, u32[]{:S(2)}) copy-start(f32[2,297]{1,0:T(2,128)} %copy-done.20) | copy-start | bytes 7132
  530.4 135.5 %all-gather.28.cloned.1.call-start = ((), (), s32[]{:S(2)}) async-start(), calls=%async_computation.16 | async-start | bytes 10543104 | tf_op jit(solution)/shard_map/all_gather | solution.py:112
  572.8 3.8 copy-start.1
  572.8 3.8 copy-start.3
  572.8 3.9 copy-start.4
  578.3 1.2 copy-start.6
Sparse Core Ops, SparseCore 0:
  12.4 33.0 all-gather.11
  107.8 43.8 reduce-scatter.4
  291.3 41.6 reduce-scatter.8
  372.4 41.1 reduce-scatter.6
  580.4 85.4 all-gather.27
Sparse Core Ops, SparseCore 1:
  110.6 42.7 all-gather.19
  156.7 31.7 all-gather.13
  190.8 40.5 all-gather.23
  233.0 31.2 all-gather.21
  266.4 40.5 all-gather.15
  309.2 40.0 all-gather.17
  417.3 31.7 all-gather.25
  530.5 42.2 reduce-scatter.10
